TPU v7x, 128 devices: a whole 4x4x4 slice. The times are simulated.
128 devices in a mesh: gx: 8 (over z_lo, y), gy: 16 (over z_hi, x, core).
Axes of the slice: x: 4, y: 4, z: 4 (z_hi: 2, z_lo: 2; z = z_hi * 2 + z_lo), core: 2. Of those that a mesh axis runs over, the one named last changes fastest.
Arguments:
- ice_displacement: float32 [2, 64, 128, 128], P(None, 'gx', 'gy'), may hold values from -1.8 to 1.8
- ice_velocity: float32 [2, 64, 128, 128], P(None, 'gx', 'gy'), may hold values from -6 to 6
- jitter: float32 [2, 64, 128, 128], P(None, 'gx', 'gy'), may hold values from -0.2 to 0.2
- bond_mask: int32 [64, 128, 9], P('gx', 'gy'), may hold values from -2147483648 to 2147483647, as said below
- contact_node: int32 [128, 128], P('gy'), may hold values from 0 to 8388607, as said below
- intersection: float32 [128, 128], P('gy'), may hold values from -0.5 to 1
- shell_deflection: float32 [1024, 8192], P('gx', 'gy'), may hold values from -1.8 to 1.8
- shell_velocity: float32 [1024, 8192], P('gx', 'gy'), may hold values from -6 to 6
Outputs:
- ice_moved: float32 [2, 64, 128, 128], P(None, 'gx', 'gy')
- ice_speed: float32 [2, 64, 128, 128], P(None, 'gx', 'gy')
- shell_moved: float32 [1024, 8192], P('gx', 'gy')
- shell_speed: float32 [1024, 8192], P('gx', 'gy')
Inputs may be any that keep to these rules, and one draw needn't show every extreme that they name: Bit 4 * i + k of bond_mask[a, b, s] (bit 31 being the sign bit) is 1 where the bonds from the points of lengthwise row i of tile (a, b) to the points q with 4 q // 128 == k of neighbouring tile s are intact. contact_node = r * 8192 + c for shell row r and column c; for point q of tile column t, c // 4 == t * 16 + q % 16 and r // 128 == q // 16.
All inputs are finite; a program needn't handle non-finite values.
Results may differ from a plain program's by a relative error of at most 0.0001.
Values sent between devices are 32-bit elements; how exact they have to be, the bound alone decides.
A program may use at most 64 MiB of HBM per device.

v0:
```python
import jax
import jax.numpy as jnp
from jax import lax
from jax.sharding import PartitionSpec as P

TILE_X = 8
TILE_Y = 16
PTS = 128
STEPS = 2
BOND_C = 1.0
HORIZON = 3.5
DELTA_SQ = 0.25
PENALTY = 4.0
BEND = 0.5
STEP_DT = 0.2


def extended(cells, sides, width):
    for axis, dim in sides:
        count = lax.axis_size(axis)
        ends = count - 1
        head = lax.slice_in_dim(cells, 0, width, axis=dim)
        tail = lax.slice_in_dim(cells, cells.shape[dim] - width, cells.shape[dim], axis=dim)
        cells = jnp.concatenate(
            [
                lax.ppermute(tail, axis, [(i, (i + 1) % count) for i in range(ends)]),
                cells,
                lax.ppermute(head, axis, [((i + 1) % count, i) for i in range(ends)]),
            ],
            axis=dim,
        )
    return cells


def spread(array, axis, root):
    mine = lax.axis_index(axis) == root
    return lax.psum(jnp.where(mine, array, jnp.zeros_like(array)), axis)


def pair_force(center, nearby, words, shift_x, shift_y):
    points = jnp.arange(TILE_X * TILE_Y, dtype=jnp.int32)
    bit_index = 4 * (points // TILE_Y)[:, None] + (4 * points // PTS)[None, :]
    intact = jnp.right_shift(words[..., None, None], bit_index) & 1
    lengthwise = (points // TILE_Y).astype(jnp.float32)
    sideways = (points % TILE_Y).astype(jnp.float32)
    base_x = shift_x * TILE_X + lengthwise[None, :] - lengthwise[:, None]
    base_y = shift_y * TILE_Y + sideways[None, :] - sideways[:, None]
    rest_x = base_x + (nearby[2][..., None, :] - center[2][..., :, None])
    rest_y = base_y + (nearby[3][..., None, :] - center[3][..., :, None])
    now_x = rest_x + (nearby[0][..., None, :] - center[0][..., :, None])
    now_y = rest_y + (nearby[1][..., None, :] - center[1][..., :, None])
    radius = jnp.sqrt(rest_x * rest_x + rest_y * rest_y + DELTA_SQ)
    stretched = jnp.sqrt(now_x * now_x + now_y * now_y + DELTA_SQ)
    reach = jnp.maximum(1.0 - radius / HORIZON, 0.0)
    factor = (
        BOND_C
        * intact.astype(jnp.float32)
        * reach
        * reach
        * (stretched - radius)
        / (radius * stretched)
    )
    return jnp.stack([jnp.sum(factor * now_x, axis=-1), jnp.sum(factor * now_y, axis=-1)])


def ice_forces(displacement, jitter_padded, bond_mask):
    tiles_x = displacement.shape[1]
    tiles_y = displacement.shape[2]
    moved_padded = extended(displacement, (("gx", 1), ("gy", 2)), 1)
    padded = jnp.concatenate([moved_padded, jitter_padded], axis=0)
    row_ids = lax.axis_index("gx") * tiles_x + jnp.arange(-1, tiles_x + 1, dtype=jnp.int32)
    col_ids = lax.axis_index("gy") * tiles_y + jnp.arange(-1, tiles_y + 1, dtype=jnp.int32)
    rows_ok = ((row_ids >= 0) & (row_ids < tiles_x * lax.axis_size("gx"))).astype(jnp.float32)
    cols_ok = ((col_ids >= 0) & (col_ids < tiles_y * lax.axis_size("gy"))).astype(jnp.float32)
    present = rows_ok[:, None] * cols_ok[None, :]
    center = padded[:, 1 : 1 + tiles_x, 1 : 1 + tiles_y]
    totals = jnp.zeros((2, tiles_x, tiles_y, displacement.shape[3]), jnp.float32)
    for offset in range(9):
        shift_x = offset // 3 - 1
        shift_y = offset % 3 - 1
        nearby = padded[:, 1 + shift_x : 1 + shift_x + tiles_x, 1 + shift_y : 1 + shift_y + tiles_y]
        weight = present[1 + shift_x : 1 + shift_x + tiles_x, 1 + shift_y : 1 + shift_y + tiles_y]
        totals = (
            totals
            + pair_force(center, nearby, bond_mask[:, :, offset], shift_x, shift_y)
            * weight[None, :, :, None]
        )
    return totals


def laplace(field):
    return (
        field[2:, 1:-1]
        + field[:-2, 1:-1]
        + field[1:-1, 2:]
        + field[1:-1, :-2]
        - 4.0 * field[1:-1, 1:-1]
    )


def on_device(
    ice_displacement,
    ice_velocity,
    jitter,
    bond_mask,
    contact_node,
    intersection,
    shell_deflection,
    shell_velocity,
):
    shell_rows = shell_deflection.shape[0]
    shell_cols = shell_deflection.shape[1]
    node_count = shell_rows * shell_cols
    width_all = shell_cols * lax.axis_size("gy")
    row_of = contact_node // width_all
    col_of = contact_node % width_all
    owned = (row_of // shell_rows == lax.axis_index("gx")) & (
        col_of // shell_cols == lax.axis_index("gy")
    )
    local_ids = (row_of % shell_rows * shell_cols + col_of % shell_cols).reshape(-1)
    front_flag = (lax.axis_index("gx") == lax.axis_size("gx") - 1).astype(jnp.float32)
    jitter_padded = extended(jitter, (("gx", 1), ("gy", 2)), 1)
    for iteration in range(STEPS):
        forces = ice_forces(ice_displacement, jitter_padded, bond_mask)
        front_gap = ice_displacement[0, -1] + intersection
        gaps = spread(front_gap, "gx", lax.axis_size("gx") - 1)
        reached = shell_deflection.reshape(-1)[local_ids].reshape(gaps.shape)
        pushes = jnp.where(owned, PENALTY * jnp.maximum(gaps - reached, 0.0), 0.0)
        loading = jax.ops.segment_sum(pushes.reshape(-1), local_ids, num_segments=node_count)
        loading = loading.reshape(shell_rows, shell_cols)
        my_pushes = lax.psum(pushes, "gx") * front_flag
        forces = forces.at[0, -1].add(-my_pushes)
        shell_padded = extended(shell_deflection, (("gx", 0), ("gy", 1)), 2)
        bending = laplace(laplace(shell_padded))
        ice_velocity = ice_velocity + STEP_DT * forces
        ice_displacement = ice_displacement + STEP_DT * ice_velocity
        shell_velocity = shell_velocity + STEP_DT * (loading - BEND * bending)
        shell_deflection = shell_deflection + STEP_DT * shell_velocity
    return (ice_displacement, ice_velocity, shell_deflection, shell_velocity)


def solution(mesh):
    in_specs = (
        P(None, "gx", "gy", None),
        P(None, "gx", "gy", None),
        P(None, "gx", "gy", None),
        P("gx", "gy", None),
        P("gy", None),
        P("gy", None),
        P("gx", "gy"),
        P("gx", "gy"),
    )
    out_specs = (P(None, "gx", "gy", None), P(None, "gx", "gy", None), P("gx", "gy"), P("gx", "gy"))
    return jax.shard_map(
        on_device, mesh=mesh, in_specs=in_specs, out_specs=out_specs, check_vma=False
    )
```

profile of v0, /device:TPU:47, one launch (start us, length us, event | category | flops | bytes accessed | tf_op | source)
XLA Modules:
  0.0 394.4 jit_solution(1697325926070671556)
XLA Ops:
  19.4 15.6 %psum.28 = f32[8,128]{1,0:T(8,128)S(1)} all-reduce(f32[8,128]{1,0:T(8,128)S(1)} %fusion.96), channel_id=1, replica_groups=mesh['gx'=8,'gy'=16] {'gx'}, use_global_device_ids=true, to_apply=%region_19.20 | all-reduce | flops 1024 | bytes 8192 | tf_op jit(solution)/shard_map/psum | solution.py:37
  35.2 6.2 %gather_fusion = f32[1024]{0:T(1024)S(1)} fusion(f32[65536]{0:T(1024)S(1)} %bitcast.195, s32[1024]{0:T(1024)S(1)} %broadcast_clamp_fusion), kind=kCustom, calls=%fused_computation | custom fusion | bytes 12288 | tf_op jit(solution)/shard_map/gather | solution.py:127
  42.3 11.0 %multiply_reduce_fusion.27 = (f32[8,8,128]{2,1,0:T(8,128)S(1)}, f32[8,8,128]{2,1,0:T(8,128)S(1)}) fusion(f32[8,8,128]{2,1,0:T(8,128)S(1)} %get-tuple-element.167, f32[8,8,128]{2,1,0:T(8,128)S(1)} %get-tuple-element.165, f32[128,128]{1,0:T(8,128)S(1)} %get-tuple-element.200, f32[8,8,128]{2,1,0:T(8,128)S(1)} %get-tuple-element.166, ...), kind=kLoop, calls=%fused_computation.95 | loop fusion | flops 33538048 | bytes 393472 | tf_op jit(solution)/shard_map/reduce_sum | solution.py:63
  53.3 16.0 %psum.29 = f32[8,128]{1,0:T(8,128)S(1)} all-reduce(f32[8,128]{1,0:T(8,128)S(1)} %get-tuple-element.86), channel_id=1, replica_groups=mesh['gx'=8,'gy'=16] {'gx'}, use_global_device_ids=true, to_apply=%region_20.21 | all-reduce | flops 1024 | bytes 8192 | tf_op jit(solution)/shard_map/psum | solution.py:131
  69.4 11.5 %collective-permute-start.15 = (f32[132,2]{1,0:T(8,128)S(1)}, f32[132,2]{1,0:T(8,128)S(1)}, u32[]{:S(2)}, u32[]{:S(2)}) collective-permute-start(f32[132,2]{1,0:T(8,128)S(1)} %get-tuple-element.91), channel_id=1, source_target_pairs={{1,0},{2,1},{3,2},{4,3},{5,4},{6,5},{7,6},{8,7},{9,8},{10,9},{11,1... | collective-permute-start | bytes 3176 | tf_op jit(solution)/shard_map/ppermute | solution.py:28
  81.1 4.4 %collective-permute-start.14 = (f32[132,2]{1,0:T(8,128)S(1)}, f32[132,2]{1,0:T(8,128)S(1)}, u32[]{:S(2)}, u32[]{:S(2)}) collective-permute-start(f32[132,2]{1,0:T(8,128)S(1)} %get-tuple-element.90), channel_id=1, source_target_pairs={{0,1},{1,2},{2,3},{3,4},{4,5},{5,6},{6,7},{7,8},{8,9},{9,10},{10,1... | collective-permute-start | bytes 3176 | tf_op jit(solution)/shard_map/ppermute | solution.py:26
  86.3 6.0 %scatter_custom_fusion = f32[65536]{0:T(1024)S(1)} fusion(s32[1024]{0:T(1024)S(1)} %fusion.119, f32[1024]{0:T(1024)S(1)} %bitcast.238, f32[]{:T(128)} %constant.364.clone.1), kind=kCustom, calls=%fused_computation.227 | custom fusion | flops 1024 | bytes 262148 | tf_op jit(solution)/shard_map/scatter-add | solution.py:129
  95.9 6.2 %gather_fusion.1 = f32[1024]{0:T(1024)S(1)} fusion(f32[65536]{0:T(1024)S(1)} %bitcast.196, s32[1024]{0:T(1024)S(1)} %broadcast_clamp_fusion), kind=kCustom, calls=%fused_computation.1 | custom fusion | bytes 12288 | tf_op jit(solution)/shard_map/gather | solution.py:127
  112.2 7.3 %collective-permute-start.5 = (f32[2,10,1,128]{3,2,1,0:T(1,128)S(1)}, f32[2,10,1,128]{3,2,1,0:T(1,128)S(1)}, u32[]{:S(2)}, u32[]{:S(2)}) collective-permute-start(f32[2,10,1,128]{3,2,1,0:T(1,128)S(1)} %get-tuple-element.138), channel_id=1, source_target_pairs={{0,1},{1,2},{2,3},{3,4},{4,5},{5,6},{6,7},{7,8},{8,9},{9,10},{10,1... | collective-permute-start | bytes 30728 | tf_op jit(solution)/shard_map/ppermute | solution.py:26
  121.5 7.5 %collective-permute-start.18 = (f32[132,2]{1,0:T(8,128)S(1)}, f32[132,2]{1,0:T(8,128)S(1)}, u32[]{:S(2)}, u32[]{:S(2)}) collective-permute-start(f32[132,2]{1,0:T(8,128)S(1)} %get-tuple-element.88), channel_id=1, source_target_pairs={{0,1},{1,2},{2,3},{3,4},{4,5},{5,6},{6,7},{7,8},{8,9},{9,10},{10,1... | collective-permute-start | bytes 3176 | tf_op jit(solution)/shard_map/ppermute | solution.py:26
  129.0 21.8 %multiply_reduce_fusion.21 = (f32[8,8,128]{2,1,0:T(8,128)S(1)}, f32[8,8,128]{2,1,0:T(8,128)S(1)}, f32[8,8,128]{2,1,0:T(8,128)S(1)}, f32[8,8,128]{2,1,0:T(8,128)S(1)}) fusion(f32[8,8,128]{2,1,0:T(8,128)S(1)} %get-tuple-element.151, f32[8,8,128]{2,1,0:T(8,128)S(1)} %get-tuple-element.149, f32[128,128]{1,0:T(8,128)S(1)} %get-tuple-element.202, ...), kind=kLoop, calls=%fused_computation.68 | loop fusion | flops 67076096 | bytes 786944 | tf_op jit(solution)/shard_map/reduce_sum | solution.py:63
  154.0 21.8 %multiply_reduce_fusion.23 = (f32[8,8,128]{2,1,0:T(8,128)S(1)}, f32[8,8,128]{2,1,0:T(8,128)S(1)}, f32[8,8,128]{2,1,0:T(8,128)S(1)}, f32[8,8,128]{2,1,0:T(8,128)S(1)}) fusion(f32[8,8,128]{2,1,0:T(8,128)S(1)} %get-tuple-element.131, f32[8,8,128]{2,1,0:T(8,128)S(1)} %get-tuple-element.125, f32[128,128]{1,0:T(8,128)S(1)} %get-tuple-element.202, ...), kind=kLoop, calls=%fused_computation.77 | loop fusion | flops 67076096 | bytes 786944 | tf_op jit(solution)/shard_map/reduce_sum | solution.py:63
  175.9 21.8 %multiply_reduce_fusion.31 = (f32[8,8,128]{2,1,0:T(8,128)S(1)}, f32[8,8,128]{2,1,0:T(8,128)S(1)}, f32[8,8,128]{2,1,0:T(8,128)S(1)}, f32[8,8,128]{2,1,0:T(8,128)S(1)}) fusion(f32[8,8,128]{2,1,0:T(8,128)S(1)} %get-tuple-element.115, f32[8,8,128]{2,1,0:T(8,128)S(1)} %get-tuple-element.109, f32[8,8,128]{2,1,0:T(8,128)S(1)} %get-tuple-element.167, ...), kind=kLoop, calls=%fused_computation.113 | loop fusion | flops 67076096 | bytes 786944 | tf_op jit(solution)/shard_map/reduce_sum | solution.py:63
  197.7 32.4 %multiply_reduce_fusion.19 = (f32[8,8,128]{2,1,0:T(8,128)S(1)}, f32[8,8,128]{2,1,0:T(8,128)S(1)}, f32[8,8,128]{2,1,0:T(8,128)S(1)}, f32[8,8,128]{2,1,0:T(8,128)S(1)}) fusion(f32[8,8,128]{2,1,0:T(8,128)S(1)} %get-tuple-element.119, f32[8,8,128]{2,1,0:T(8,128)S(1)} %get-tuple-element.113, f32[128,128]{1,0:T(8,128)S(1)} %get-tuple-element.202, ...), kind=kLoop, calls=%fused_computation.59 | loop fusion | flops 67076096 | bytes 786944 | tf_op jit(solution)/shard_map/reduce_sum | solution.py:63
  237.6 14.9 %psum.30 = f32[8,128]{1,0:T(8,128)S(1)} all-reduce(f32[8,128]{1,0:T(8,128)S(1)} %fusion.89), channel_id=1, replica_groups=mesh['gx'=8,'gy'=16] {'gx'}, use_global_device_ids=true, to_apply=%region_39.40 | all-reduce | flops 1024 | bytes 8192 | tf_op jit(solution)/shard_map/psum | solution.py:37
  252.5 6.0 %scatter_custom_fusion.1 = f32[65536]{0:T(1024)S(1)} fusion(s32[1024]{0:T(1024)S(1)} %fusion.119, f32[1024]{0:T(1024)S(1)} %bitcast.236, f32[]{:T(128)} %constant.364.clone.1), kind=kCustom, calls=%fused_computation.225 | custom fusion | flops 1024 | bytes 262148 | tf_op jit(solution)/shard_map/scatter-add | solution.py:129
  259.7 15.9 %psum.31 = f32[8,128]{1,0:T(8,128)S(1)} all-reduce(f32[8,128]{1,0:T(8,128)S(1)} %fusion.92), channel_id=1, replica_groups=mesh['gx'=8,'gy'=16] {'gx'}, use_global_device_ids=true, to_apply=%region_41.42 | all-reduce | flops 1024 | bytes 8192 | tf_op jit(solution)/shard_map/psum | solution.py:131
  275.7 10.1 %collective-permute-start.11 = (f32[2,10,1,128]{3,2,1,0:T(1,128)S(1)}, f32[2,10,1,128]{3,2,1,0:T(1,128)S(1)}, u32[]{:S(2)}, u32[]{:S(2)}) collective-permute-start(f32[2,10,1,128]{3,2,1,0:T(1,128)S(1)} %get-tuple-element.134), channel_id=1, source_target_pairs={{1,0},{2,1},{3,2},{4,3},{5,4},{6,5},{7,6},{8,7},{9,8},{10,9},{11,1... | collective-permute-start | bytes 30728 | tf_op jit(solution)/shard_map/ppermute | solution.py:28
  285.8 6.5 %collective-permute-start.10 = (f32[2,10,1,128]{3,2,1,0:T(1,128)S(1)}, f32[2,10,1,128]{3,2,1,0:T(1,128)S(1)}, u32[]{:S(2)}, u32[]{:S(2)}) collective-permute-start(f32[2,10,1,128]{3,2,1,0:T(1,128)S(1)} %get-tuple-element.135), channel_id=1, source_target_pairs={{0,1},{1,2},{2,3},{3,4},{4,5},{5,6},{6,7},{7,8},{8,9},{9,10},{10,1... | collective-permute-start | bytes 30728 | tf_op jit(solution)/shard_map/ppermute | solution.py:26
  292.3 21.7 %multiply_reduce_fusion.9 = (f32[8,8,128]{2,1,0:T(8,128)S(1)}, f32[8,8,128]{2,1,0:T(8,128)S(1)}, f32[8,8,128]{2,1,0:T(8,128)S(1)}, f32[8,8,128]{2,1,0:T(8,128)S(1)}) fusion(f32[8,8,128]{2,1,0:T(8,128)S(1)} %get-tuple-element.155, f32[8,8,128]{2,1,0:T(8,128)S(1)} %get-tuple-element.165, f32[128,128]{1,0:T(8,128)S(1)} %get-tuple-element.200, ...), kind=kLoop, calls=%fused_computation.34 | loop fusion | flops 67076096 | bytes 655872 | tf_op jit(solution)/shard_map/reduce_sum | solution.py:63
  314.2 11.1 %multiply_reduce_fusion.17 = (f32[8,8,128]{2,1,0:T(8,128)S(1)}, f32[8,8,128]{2,1,0:T(8,128)S(1)}) fusion(f32[8,8,128]{2,1,0:T(8,128)S(1)} %get-tuple-element.155, f32[8,8,128]{2,1,0:T(8,128)S(1)} %get-tuple-element.107, f32[8,8,128]{2,1,0:T(8,128)S(1)} %get-tuple-element.165, f32[8,8,128]{2,1,0:T(8,128)S(1)} %get-tuple-element.121, ...), kind=kLoop, calls=%fused_computation.54 | loop fusion | flops 33538048 | bytes 524544 | tf_op jit(solution)/shard_map/reduce_sum | solution.py:63
  325.3 22.0 %multiply_reduce_fusion.7 = (f32[8,8,128]{2,1,0:T(8,128)S(1)}, f32[8,8,128]{2,1,0:T(8,128)S(1)}, f32[8,8,128]{2,1,0:T(8,128)S(1)}, f32[8,8,128]{2,1,0:T(8,128)S(1)}) fusion(f32[8,8,128]{2,1,0:T(8,128)S(1)} %get-tuple-element.99, f32[8,8,128]{2,1,0:T(8,128)S(1)} %get-tuple-element.155, f32[8,8,128]{2,1,0:T(8,128)S(1)} %get-tuple-element.108, ...), kind=kLoop, calls=%fused_computation.29 | loop fusion | flops 67076096 | bytes 786944 | tf_op jit(solution)/shard_map/reduce_sum | solution.py:63
  347.3 21.8 %multiply_reduce_fusion.5 = (f32[8,8,128]{2,1,0:T(8,128)S(1)}, f32[8,8,128]{2,1,0:T(8,128)S(1)}, f32[8,8,128]{2,1,0:T(8,128)S(1)}, f32[8,8,128]{2,1,0:T(8,128)S(1)}) fusion(f32[8,8,128]{2,1,0:T(8,128)S(1)} %get-tuple-element.104, f32[8,8,128]{2,1,0:T(8,128)S(1)} %get-tuple-element.155, f32[8,8,128]{2,1,0:T(8,128)S(1)} %get-tuple-element.125, ...), kind=kLoop, calls=%fused_computation.24 | loop fusion | flops 67076096 | bytes 786944 | tf_op jit(solution)/shard_map/reduce_sum | solution.py:63
  369.1 22.0 %multiply_reduce_fusion.1 = (f32[8,8,128]{2,1,0:T(8,128)S(1)}, f32[8,8,128]{2,1,0:T(8,128)S(1)}, f32[8,8,128]{2,1,0:T(8,128)S(1)}, f32[8,8,128]{2,1,0:T(8,128)S(1)}) fusion(f32[8,8,128]{2,1,0:T(8,128)S(1)} %get-tuple-element.97, f32[8,8,128]{2,1,0:T(8,128)S(1)} %get-tuple-element.155, f32[8,8,128]{2,1,0:T(8,128)S(1)} %get-tuple-element.113, ...), kind=kLoop, calls=%fused_computation.14 | loop fusion | flops 67076096 | bytes 786944 | tf_op jit(solution)/shard_map/reduce_sum | solution.py:63
  (129 shorter events, 51.0 us)
Async XLA Ops:
  0.6 17.6 %copy-start.6 = (s32[8,128]{1,0:T(8,128)S(1)}, s32[8,128]{1,0:T(8,128)}, u32[]{:S(2)}) copy-start(s32[8,128]{1,0:T(8,128)} %param.16) | copy-start | bytes 12292
  0.6 17.7 %copy-start.1 = (s32[8,8,9]{2,1,0:T(8,128)S(1)}, s32[8,8,9]{2,1,0:T(8,128)}, u32[]{:S(2)}) copy-start(s32[8,8,9]{2,1,0:T(8,128)} %param.15) | copy-start | bytes 6916
  1.4 104.8 %collective-permute-start.3 = (f32[2,1,8,128]{3,2,1,0:T(8,128)S(1)}, f32[2,1,8,128]{3,2,1,0:T(8,128)S(1)}, u32[]{:S(2)}, u32[]{:S(2)}) collective-permute-start(f32[2,1,8,128]{3,2,1,0:T(8,128)S(1)} %get-tuple-element.171), channel_id=1, source_target_pairs={{0,16},{16,32},{32,48},{48,64},{64,80},{80,96},{96,112},{1,17},{17... | collective-permute-start | bytes 24584 | tf_op jit(solution)/shard_map/ppermute | solution.py:26
  4.6 103.6 %collective-permute-start.4 = (f32[2,1,8,128]{3,2,1,0:T(8,128)S(1)}, f32[2,1,8,128]{3,2,1,0:T(8,128)S(1)}, u32[]{:S(2)}, u32[]{:S(2)}) collective-permute-start(f32[2,1,8,128]{3,2,1,0:T(8,128)S(1)} %get-tuple-element.170), channel_id=1, source_target_pairs={{16,0},{32,16},{48,32},{64,48},{80,64},{96,80},{112,96},{17,1},{33... | collective-permute-start | bytes 24584 | tf_op jit(solution)/shard_map/ppermute | solution.py:28
  7.4 102.8 %collective-permute-start = (f32[2,1,8,128]{3,2,1,0:T(8,128)S(1)}, f32[2,1,8,128]{3,2,1,0:T(8,128)S(1)}, u32[]{:S(2)}, u32[]{:S(2)}) collective-permute-start(f32[2,1,8,128]{3,2,1,0:T(8,128)S(1)} %get-tuple-element.169), channel_id=1, source_target_pairs={{0,16},{16,32},{32,48},{48,64},{64,80},{80,96},{96,112},{1,17},{17... | collective-permute-start | bytes 24584 | tf_op jit(solution)/shard_map/ppermute | solution.py:26
  11.3 58.0 %collective-permute-start.13 = (f32[2,512]{1,0:T(2,128)S(1)}, f32[2,512]{1,0:T(2,128)S(1)}, u32[]{:S(2)}, u32[]{:S(2)}) collective-permute-start(f32[2,512]{1,0:T(2,128)S(1)} %get-tuple-element.95), channel_id=1, source_target_pairs={{16,0},{32,16},{48,32},{64,48},{80,64},{96,80},{112,96},{17,1},{33... | collective-permute-start | bytes 12296 | tf_op jit(solution)/shard_map/ppermute | solution.py:28
  14.2 55.1 %collective-permute-start.12 = (f32[2,512]{1,0:T(2,128)S(1)}, f32[2,512]{1,0:T(2,128)S(1)}, u32[]{:S(2)}, u32[]{:S(2)}) collective-permute-start(f32[2,512]{1,0:T(2,128)S(1)} %get-tuple-element.94), channel_id=1, source_target_pairs={{0,16},{16,32},{32,48},{48,64},{64,80},{80,96},{96,112},{1,17},{17... | collective-permute-start | bytes 12296 | tf_op jit(solution)/shard_map/ppermute | solution.py:26
  18.3 16.6 %copy-start = (f32[128,512]{1,0:T(8,128)S(1)}, f32[128,512]{1,0:T(8,128)}, u32[]{:S(2)}) copy-start(f32[128,512]{1,0:T(8,128)} %param.18) | copy-start | bytes 786436
  69.4 22.9 %collective-permute-start.15 = (f32[132,2]{1,0:T(8,128)S(1)}, f32[132,2]{1,0:T(8,128)S(1)}, u32[]{:S(2)}, u32[]{:S(2)}) collective-permute-start(f32[132,2]{1,0:T(8,128)S(1)} %get-tuple-element.91), channel_id=1, source_target_pairs={{1,0},{2,1},{3,2},{4,3},{5,4},{6,5},{7,6},{8,7},{9,8},{10,9},{11,1... | collective-permute-start | bytes 3176 | tf_op jit(solution)/shard_map/ppermute | solution.py:28
  81.1 13.3 %collective-permute-start.14 = (f32[132,2]{1,0:T(8,128)S(1)}, f32[132,2]{1,0:T(8,128)S(1)}, u32[]{:S(2)}, u32[]{:S(2)}) collective-permute-start(f32[132,2]{1,0:T(8,128)S(1)} %get-tuple-element.90), channel_id=1, source_target_pairs={{0,1},{1,2},{2,3},{3,4},{4,5},{5,6},{6,7},{7,8},{8,9},{9,10},{10,1... | collective-permute-start | bytes 3176 | tf_op jit(solution)/shard_map/ppermute | solution.py:26
  92.4 17.8 %collective-permute-start.1 = (f32[2,1,8,128]{3,2,1,0:T(8,128)S(1)}, f32[2,1,8,128]{3,2,1,0:T(8,128)S(1)}, u32[]{:S(2)}, u32[]{:S(2)}) collective-permute-start(f32[2,1,8,128]{3,2,1,0:T(8,128)S(1)} %get-tuple-element.168), channel_id=1, source_target_pairs={{16,0},{32,16},{48,32},{64,48},{80,64},{96,80},{112,96},{17,1},{33... | collective-permute-start | bytes 24584 | tf_op jit(solution)/shard_map/ppermute | solution.py:28
  102.1 8.1 %copy-start.3 = (f32[2,8,8,128]{3,2,1,0:T(8,128)S(1)}, f32[2,8,8,128]{3,2,1,0:T(8,128)}, u32[]{:S(2)}) copy-start(f32[2,8,8,128]{3,2,1,0:T(8,128)} %param.14) | copy-start | bytes 196612
  102.1 17.4 %collective-permute-start.17 = (f32[2,512]{1,0:T(2,128)S(1)}, f32[2,512]{1,0:T(2,128)S(1)}, u32[]{:S(2)}, u32[]{:S(2)}) collective-permute-start(f32[2,512]{1,0:T(2,128)S(1)} %get-tuple-element.93), channel_id=1, source_target_pairs={{16,0},{32,16},{48,32},{64,48},{80,64},{96,80},{112,96},{17,1},{33... | collective-permute-start | bytes 12296 | tf_op jit(solution)/shard_map/ppermute | solution.py:28
  106.2 13.3 %collective-permute-start.16 = (f32[2,512]{1,0:T(2,128)S(1)}, f32[2,512]{1,0:T(2,128)S(1)}, u32[]{:S(2)}, u32[]{:S(2)}) collective-permute-start(f32[2,512]{1,0:T(2,128)S(1)} %get-tuple-element.92), channel_id=1, source_target_pairs={{0,16},{16,32},{32,48},{48,64},{64,80},{80,96},{96,112},{1,17},{17... | collective-permute-start | bytes 12296 | tf_op jit(solution)/shard_map/ppermute | solution.py:26
  108.2 67.6 %collective-permute-start.7 = (f32[2,10,1,128]{3,2,1,0:T(1,128)S(1)}, f32[2,10,1,128]{3,2,1,0:T(1,128)S(1)}, u32[]{:S(2)}, u32[]{:S(2)}) collective-permute-start(f32[2,10,1,128]{3,2,1,0:T(1,128)S(1)} %get-tuple-element.139), channel_id=1, source_target_pairs={{1,0},{2,1},{3,2},{4,3},{5,4},{6,5},{7,6},{8,7},{9,8},{10,9},{11,1... | collective-permute-start | bytes 30728 | tf_op jit(solution)/shard_map/ppermute | solution.py:28
  110.3 65.6 %collective-permute-start.6 = (f32[2,10,1,128]{3,2,1,0:T(1,128)S(1)}, f32[2,10,1,128]{3,2,1,0:T(1,128)S(1)}, u32[]{:S(2)}, u32[]{:S(2)}) collective-permute-start(f32[2,10,1,128]{3,2,1,0:T(1,128)S(1)} %get-tuple-element.137), channel_id=1, source_target_pairs={{1,0},{2,1},{3,2},{4,3},{5,4},{6,5},{7,6},{8,7},{9,8},{10,9},{11,1... | collective-permute-start | bytes 30728 | tf_op jit(solution)/shard_map/ppermute | solution.py:28
  112.2 41.6 %collective-permute-start.5 = (f32[2,10,1,128]{3,2,1,0:T(1,128)S(1)}, f32[2,10,1,128]{3,2,1,0:T(1,128)S(1)}, u32[]{:S(2)}, u32[]{:S(2)}) collective-permute-start(f32[2,10,1,128]{3,2,1,0:T(1,128)S(1)} %get-tuple-element.138), channel_id=1, source_target_pairs={{0,1},{1,2},{2,3},{3,4},{4,5},{5,6},{6,7},{7,8},{8,9},{9,10},{10,1... | collective-permute-start | bytes 30728 | tf_op jit(solution)/shard_map/ppermute | solution.py:26
  119.6 31.3 %collective-permute-start.19 = (f32[132,2]{1,0:T(8,128)S(1)}, f32[132,2]{1,0:T(8,128)S(1)}, u32[]{:S(2)}, u32[]{:S(2)}) collective-permute-start(f32[132,2]{1,0:T(8,128)S(1)} %get-tuple-element.89), channel_id=1, source_target_pairs={{1,0},{2,1},{3,2},{4,3},{5,4},{6,5},{7,6},{8,7},{9,8},{10,9},{11,1... | collective-permute-start | bytes 3176 | tf_op jit(solution)/shard_map/ppermute | solution.py:28
  121.5 31.6 %collective-permute-start.18 = (f32[132,2]{1,0:T(8,128)S(1)}, f32[132,2]{1,0:T(8,128)S(1)}, u32[]{:S(2)}, u32[]{:S(2)}) collective-permute-start(f32[132,2]{1,0:T(8,128)S(1)} %get-tuple-element.88), channel_id=1, source_target_pairs={{0,1},{1,2},{2,3},{3,4},{4,5},{5,6},{6,7},{7,8},{8,9},{9,10},{10,1... | collective-permute-start | bytes 3176 | tf_op jit(solution)/shard_map/ppermute | solution.py:26
  150.9 3.1 collective-permute-start.2
  232.3 43.4 %collective-permute-start.9 = (f32[2,1,8,128]{3,2,1,0:T(8,128)S(1)}, f32[2,1,8,128]{3,2,1,0:T(8,128)S(1)}, u32[]{:S(2)}, u32[]{:S(2)}) collective-permute-start(f32[2,1,8,128]{3,2,1,0:T(8,128)S(1)} %get-tuple-element.157), channel_id=1, source_target_pairs={{16,0},{32,16},{48,32},{64,48},{80,64},{96,80},{112,96},{17,1},{33... | collective-permute-start | bytes 24584 | tf_op jit(solution)/shard_map/ppermute | solution.py:28
  235.7 40.0 %collective-permute-start.8 = (f32[2,1,8,128]{3,2,1,0:T(8,128)S(1)}, f32[2,1,8,128]{3,2,1,0:T(8,128)S(1)}, u32[]{:S(2)}, u32[]{:S(2)}) collective-permute-start(f32[2,1,8,128]{3,2,1,0:T(8,128)S(1)} %get-tuple-element.156), channel_id=1, source_target_pairs={{0,16},{16,32},{32,48},{48,64},{64,80},{80,96},{96,112},{1,17},{17... | collective-permute-start | bytes 24584 | tf_op jit(solution)/shard_map/ppermute | solution.py:26
  275.7 38.4 %collective-permute-start.11 = (f32[2,10,1,128]{3,2,1,0:T(1,128)S(1)}, f32[2,10,1,128]{3,2,1,0:T(1,128)S(1)}, u32[]{:S(2)}, u32[]{:S(2)}) collective-permute-start(f32[2,10,1,128]{3,2,1,0:T(1,128)S(1)} %get-tuple-element.134), channel_id=1, source_target_pairs={{1,0},{2,1},{3,2},{4,3},{5,4},{6,5},{7,6},{8,7},{9,8},{10,9},{11,1... | collective-permute-start | bytes 30728 | tf_op jit(solution)/shard_map/ppermute | solution.py:28
  285.8 28.3 %collective-permute-start.10 = (f32[2,10,1,128]{3,2,1,0:T(1,128)S(1)}, f32[2,10,1,128]{3,2,1,0:T(1,128)S(1)}, u32[]{:S(2)}, u32[]{:S(2)}) collective-permute-start(f32[2,10,1,128]{3,2,1,0:T(1,128)S(1)} %get-tuple-element.135), channel_id=1, source_target_pairs={{0,1},{1,2},{2,3},{3,4},{4,5},{5,6},{6,7},{7,8},{8,9},{9,10},{10,1... | collective-permute-start | bytes 30728 | tf_op jit(solution)/shard_map/ppermute | solution.py:26
  (5 other events, 11.4 us)
where the time goes:
time: 401 us; the launch traced here: 394 us
  other arithmetic  229 us (57%)
  starting transfers between devices  82.2 us (20%)
  blocking collectives  62.5 us (16%)
  local copies, waits for them, and re-layouts  18.8 us (5%)
    reduce_sum x10, other arithmetic, pair_force(): jnp.sum(factor * now_x, axis=-1)  207 us
    ppermute x10, starting transfers between devices, extended(): lax.ppermute(head, axis, [((i + 1) % count, i) for i in range(ends)])  41.7 us
    ppermute x10, starting transfers between devices, extended(): lax.ppermute(tail, axis, [(i, (i + 1) % count) for i in range(ends)])  40.4 us
    psum x2, blocking collectives, on_device(): my_pushes = lax.psum(pushes, 'gx') * front_flag  32 us
    psum x2, blocking collectives, spread(): return lax.psum(jnp.where(mine, array, jnp.zeros_like(array)), axis)  30.5 us
    gather x2, local copies, waits for them, and re-layouts, on_device(): reached = shell_deflection.reshape(-1)[local_ids].reshape(gaps.shape)  12.3 us
    scatter-add x2, other arithmetic, on_device(): jax.ops.segment_sum(pushes.reshape(-1), local_ids, num_segments=node_count)  12 us
  transfers between devices with their start and end apart: 20, of which 1 were waited for; matrix products, arithmetic and copies ran while one was open for 28% of the time, Pallas kernels for 0%

commit v1 on v0

--- a/solution.py
+++ b/solution.py
@@ -128,7 +128,7 @@
         pushes = jnp.where(owned, PENALTY * jnp.maximum(gaps - reached, 0.0), 0.0)
         loading = jax.ops.segment_sum(pushes.reshape(-1), local_ids, num_segments=node_count)
         loading = loading.reshape(shell_rows, shell_cols)
-        my_pushes = lax.psum(pushes, "gx") * front_flag
+        my_pushes = jax.lax.all_gather(pushes, "gx").sum(axis=0) * front_flag
         forces = forces.at[0, -1].add(-my_pushes)
         shell_padded = extended(shell_deflection, (("gx", 0), ("gy", 1)), 2)
         bending = laplace(laplace(shell_padded))

time: 401 us -> 425 us (1.060)
  the two profiles are of different devices: /device:TPU:47 before, /device:TPU:39 now
where the time goes in v1:
time: 425 us; the launch traced here: 419 us
  other arithmetic  229 us (54%)
  starting transfers between devices  92.7 us (22%)
  blocking collectives  75.8 us (18%)
  local copies, waits for them, and re-layouts  19.2 us (5%)
    reduce_sum x10, other arithmetic, pair_force(): jnp.sum(factor * now_x, axis=-1)  207 us
    ppermute x10, starting transfers between devices, extended(): lax.ppermute(head, axis, [((i + 1) % count, i) for i in range(ends)])  54 us
    all_gather x2, blocking collectives, on_device(): my_pushes = jax.lax.all_gather(pushes, 'gx').sum(axis=0) * front_flag  43.8 us
    ppermute x10, starting transfers between devices, extended(): lax.ppermute(tail, axis, [(i, (i + 1) % count) for i in range(ends)])  38.7 us
    psum x2, blocking collectives, spread(): return lax.psum(jnp.where(mine, array, jnp.zeros_like(array)), axis)  32.1 us
    gather x2, local copies, waits for them, and re-layouts, on_device(): reached = shell_deflection.reshape(-1)[local_ids].reshape(gaps.shape)  12.3 us
    scatter-add x2, other arithmetic, on_device(): jax.ops.segment_sum(pushes.reshape(-1), local_ids, num_segments=node_count)  12 us
  transfers between devices with their start and end apart: 20, of which 1 were waited for; matrix products, arithmetic and copies ran while one was open for 26% of the time, Pallas kernels for 0%

profile of v1, /device:TPU:39, one launch (start us, length us, event | category | flops | bytes accessed | tf_op | source)
XLA Modules:
  0.0 418.7 jit_solution(12512808589588202777)
XLA Ops:
  22.1 16.0 %psum.14 = f32[8,128]{1,0:T(8,128)S(1)} all-reduce(f32[8,128]{1,0:T(8,128)S(1)} %fusion.96), channel_id=1, replica_groups=mesh['gx'=8,'gy'=16] {'gx'}, use_global_device_ids=true, to_apply=%region_19.20 | all-reduce | flops 1024 | bytes 8192 | tf_op jit(solution)/shard_map/psum | solution.py:37
  38.2 6.2 %gather_fusion = f32[1024]{0:T(1024)S(1)} fusion(f32[65536]{0:T(1024)S(1)} %bitcast.199, s32[1024]{0:T(1024)S(1)} %broadcast_clamp_fusion), kind=kCustom, calls=%fused_computation | custom fusion | bytes 12288 | tf_op jit(solution)/shard_map/gather | solution.py:127
  44.4 21.9 %all-gather = f32[64,128]{1,0:T(8,128)S(1)} all-gather(f32[8,128]{1,0:T(8,128)S(1)} %get-tuple-element.86), channel_id=2, replica_groups=mesh['gx'=8,'gy'=16] {'gx'}, dimensions={0}, use_global_device_ids=true | all-gather | bytes 36864 | tf_op jit(solution)/shard_map/all_gather | solution.py:131
  67.4 10.9 %multiply_reduce_fusion.27 = (f32[8,8,128]{2,1,0:T(8,128)S(1)}, f32[8,8,128]{2,1,0:T(8,128)S(1)}) fusion(f32[8,8,128]{2,1,0:T(8,128)S(1)} %get-tuple-element.167, f32[8,8,128]{2,1,0:T(8,128)S(1)} %get-tuple-element.165, f32[128,128]{1,0:T(8,128)S(1)} %get-tuple-element.200, f32[8,8,128]{2,1,0:T(8,128)S(1)} %get-tuple-element.166, ...), kind=kLoop, calls=%fused_computation.95 | loop fusion | flops 33538048 | bytes 393472 | tf_op jit(solution)/shard_map/reduce_sum | solution.py:63
  79.0 14.1 %collective-permute-start.15 = (f32[132,2]{1,0:T(8,128)S(1)}, f32[132,2]{1,0:T(8,128)S(1)}, u32[]{:S(2)}, u32[]{:S(2)}) collective-permute-start(f32[132,2]{1,0:T(8,128)S(1)} %get-tuple-element.91), channel_id=1, source_target_pairs={{1,0},{2,1},{3,2},{4,3},{5,4},{6,5},{7,6},{8,7},{9,8},{10,9},{11,1... | collective-permute-start | bytes 3176 | tf_op jit(solution)/shard_map/ppermute | solution.py:28
  98.5 6.0 %scatter_custom_fusion = f32[65536]{0:T(1024)S(1)} fusion(s32[1024]{0:T(1024)S(1)} %fusion.119, f32[1024]{0:T(1024)S(1)} %bitcast.240, f32[]{:T(128)} %constant.364.clone.1), kind=kCustom, calls=%fused_computation.227 | custom fusion | flops 1024 | bytes 262148 | tf_op jit(solution)/shard_map/scatter-add | solution.py:129
  108.5 6.2 %gather_fusion.1 = f32[1024]{0:T(1024)S(1)} fusion(f32[65536]{0:T(1024)S(1)} %bitcast.200, s32[1024]{0:T(1024)S(1)} %broadcast_clamp_fusion), kind=kCustom, calls=%fused_computation.1 | custom fusion | bytes 12288 | tf_op jit(solution)/shard_map/gather | solution.py:127
  124.4 7.3 %collective-permute-start.5 = (f32[2,10,1,128]{3,2,1,0:T(1,128)S(1)}, f32[2,10,1,128]{3,2,1,0:T(1,128)S(1)}, u32[]{:S(2)}, u32[]{:S(2)}) collective-permute-start(f32[2,10,1,128]{3,2,1,0:T(1,128)S(1)} %get-tuple-element.138), channel_id=1, source_target_pairs={{0,1},{1,2},{2,3},{3,4},{4,5},{5,6},{6,7},{7,8},{8,9},{9,10},{10,1... | collective-permute-start | bytes 30728 | tf_op jit(solution)/shard_map/ppermute | solution.py:26
  133.7 7.5 %collective-permute-start.18 = (f32[132,2]{1,0:T(8,128)S(1)}, f32[132,2]{1,0:T(8,128)S(1)}, u32[]{:S(2)}, u32[]{:S(2)}) collective-permute-start(f32[132,2]{1,0:T(8,128)S(1)} %get-tuple-element.88), channel_id=1, source_target_pairs={{0,1},{1,2},{2,3},{3,4},{4,5},{5,6},{6,7},{7,8},{8,9},{9,10},{10,1... | collective-permute-start | bytes 3176 | tf_op jit(solution)/shard_map/ppermute | solution.py:26
  141.2 21.8 %multiply_reduce_fusion.21 = (f32[8,8,128]{2,1,0:T(8,128)S(1)}, f32[8,8,128]{2,1,0:T(8,128)S(1)}, f32[8,8,128]{2,1,0:T(8,128)S(1)}, f32[8,8,128]{2,1,0:T(8,128)S(1)}) fusion(f32[8,8,128]{2,1,0:T(8,128)S(1)} %get-tuple-element.151, f32[8,8,128]{2,1,0:T(8,128)S(1)} %get-tuple-element.149, f32[128,128]{1,0:T(8,128)S(1)} %get-tuple-element.202, ...), kind=kLoop, calls=%fused_computation.68 | loop fusion | flops 67076096 | bytes 786944 | tf_op jit(solution)/shard_map/reduce_sum | solution.py:63
  166.2 21.8 %multiply_reduce_fusion.23 = (f32[8,8,128]{2,1,0:T(8,128)S(1)}, f32[8,8,128]{2,1,0:T(8,128)S(1)}, f32[8,8,128]{2,1,0:T(8,128)S(1)}, f32[8,8,128]{2,1,0:T(8,128)S(1)}) fusion(f32[8,8,128]{2,1,0:T(8,128)S(1)} %get-tuple-element.131, f32[8,8,128]{2,1,0:T(8,128)S(1)} %get-tuple-element.125, f32[128,128]{1,0:T(8,128)S(1)} %get-tuple-element.202, ...), kind=kLoop, calls=%fused_computation.77 | loop fusion | flops 67076096 | bytes 786944 | tf_op jit(solution)/shard_map/reduce_sum | solution.py:63
  188.1 21.8 %multiply_reduce_fusion.31 = (f32[8,8,128]{2,1,0:T(8,128)S(1)}, f32[8,8,128]{2,1,0:T(8,128)S(1)}, f32[8,8,128]{2,1,0:T(8,128)S(1)}, f32[8,8,128]{2,1,0:T(8,128)S(1)}) fusion(f32[8,8,128]{2,1,0:T(8,128)S(1)} %get-tuple-element.115, f32[8,8,128]{2,1,0:T(8,128)S(1)} %get-tuple-element.109, f32[8,8,128]{2,1,0:T(8,128)S(1)} %get-tuple-element.167, ...), kind=kLoop, calls=%fused_computation.113 | loop fusion | flops 67076096 | bytes 786944 | tf_op jit(solution)/shard_map/reduce_sum | solution.py:63
  209.9 32.4 %multiply_reduce_fusion.19 = (f32[8,8,128]{2,1,0:T(8,128)S(1)}, f32[8,8,128]{2,1,0:T(8,128)S(1)}, f32[8,8,128]{2,1,0:T(8,128)S(1)}, f32[8,8,128]{2,1,0:T(8,128)S(1)}) fusion(f32[8,8,128]{2,1,0:T(8,128)S(1)} %get-tuple-element.119, f32[8,8,128]{2,1,0:T(8,128)S(1)} %get-tuple-element.113, f32[128,128]{1,0:T(8,128)S(1)} %get-tuple-element.202, ...), kind=kLoop, calls=%fused_computation.59 | loop fusion | flops 67076096 | bytes 786944 | tf_op jit(solution)/shard_map/reduce_sum | solution.py:63
  244.5 5.5 %collective-permute-start.9 = (f32[2,1,8,128]{3,2,1,0:T(8,128)S(1)}, f32[2,1,8,128]{3,2,1,0:T(8,128)S(1)}, u32[]{:S(2)}, u32[]{:S(2)}) collective-permute-start(f32[2,1,8,128]{3,2,1,0:T(8,128)S(1)} %get-tuple-element.157), channel_id=1, source_target_pairs={{16,0},{32,16},{48,32},{64,48},{80,64},{96,80},{112,96},{17,1},{33... | collective-permute-start | bytes 24584 | tf_op jit(solution)/shard_map/ppermute | solution.py:28
  251.9 16.0 %psum.15 = f32[8,128]{1,0:T(8,128)S(1)} all-reduce(f32[8,128]{1,0:T(8,128)S(1)} %fusion.89), channel_id=1, replica_groups=mesh['gx'=8,'gy'=16] {'gx'}, use_global_device_ids=true, to_apply=%region_39.40 | all-reduce | flops 1024 | bytes 8192 | tf_op jit(solution)/shard_map/psum | solution.py:37
  268.0 21.9 %all-gather.1 = f32[64,128]{1,0:T(8,128)S(1)} all-gather(f32[8,128]{1,0:T(8,128)S(1)} %fusion.92), channel_id=3, replica_groups=mesh['gx'=8,'gy'=16] {'gx'}, dimensions={0}, use_global_device_ids=true | all-gather | bytes 36864 | tf_op jit(solution)/shard_map/all_gather | solution.py:131
  289.9 6.0 %scatter_custom_fusion.1 = f32[65536]{0:T(1024)S(1)} fusion(s32[1024]{0:T(1024)S(1)} %fusion.119, f32[1024]{0:T(1024)S(1)} %bitcast.239, f32[]{:T(128)} %constant.364.clone.1), kind=kCustom, calls=%fused_computation.225 | custom fusion | flops 1024 | bytes 262148 | tf_op jit(solution)/shard_map/scatter-add | solution.py:129
  297.1 13.0 %collective-permute-start.11 = (f32[2,10,1,128]{3,2,1,0:T(1,128)S(1)}, f32[2,10,1,128]{3,2,1,0:T(1,128)S(1)}, u32[]{:S(2)}, u32[]{:S(2)}) collective-permute-start(f32[2,10,1,128]{3,2,1,0:T(1,128)S(1)} %get-tuple-element.134), channel_id=1, source_target_pairs={{1,0},{2,1},{3,2},{4,3},{5,4},{6,5},{7,6},{8,7},{9,8},{10,9},{11,1... | collective-permute-start | bytes 30728 | tf_op jit(solution)/shard_map/ppermute | solution.py:28
  310.1 6.5 %collective-permute-start.10 = (f32[2,10,1,128]{3,2,1,0:T(1,128)S(1)}, f32[2,10,1,128]{3,2,1,0:T(1,128)S(1)}, u32[]{:S(2)}, u32[]{:S(2)}) collective-permute-start(f32[2,10,1,128]{3,2,1,0:T(1,128)S(1)} %get-tuple-element.135), channel_id=1, source_target_pairs={{0,1},{1,2},{2,3},{3,4},{4,5},{5,6},{6,7},{7,8},{8,9},{9,10},{10,1... | collective-permute-start | bytes 30728 | tf_op jit(solution)/shard_map/ppermute | solution.py:26
  316.6 21.7 %multiply_reduce_fusion.9 = (f32[8,8,128]{2,1,0:T(8,128)S(1)}, f32[8,8,128]{2,1,0:T(8,128)S(1)}, f32[8,8,128]{2,1,0:T(8,128)S(1)}, f32[8,8,128]{2,1,0:T(8,128)S(1)}) fusion(f32[8,8,128]{2,1,0:T(8,128)S(1)} %get-tuple-element.155, f32[8,8,128]{2,1,0:T(8,128)S(1)} %get-tuple-element.165, f32[128,128]{1,0:T(8,128)S(1)} %get-tuple-element.200, ...), kind=kLoop, calls=%fused_computation.34 | loop fusion | flops 67076096 | bytes 655872 | tf_op jit(solution)/shard_map/reduce_sum | solution.py:63
  338.5 11.1 %multiply_reduce_fusion.17 = (f32[8,8,128]{2,1,0:T(8,128)S(1)}, f32[8,8,128]{2,1,0:T(8,128)S(1)}) fusion(f32[8,8,128]{2,1,0:T(8,128)S(1)} %get-tuple-element.155, f32[8,8,128]{2,1,0:T(8,128)S(1)} %get-tuple-element.107, f32[8,8,128]{2,1,0:T(8,128)S(1)} %get-tuple-element.165, f32[8,8,128]{2,1,0:T(8,128)S(1)} %get-tuple-element.121, ...), kind=kLoop, calls=%fused_computation.54 | loop fusion | flops 33538048 | bytes 524544 | tf_op jit(solution)/shard_map/reduce_sum | solution.py:63
  349.6 22.0 %multiply_reduce_fusion.7 = (f32[8,8,128]{2,1,0:T(8,128)S(1)}, f32[8,8,128]{2,1,0:T(8,128)S(1)}, f32[8,8,128]{2,1,0:T(8,128)S(1)}, f32[8,8,128]{2,1,0:T(8,128)S(1)}) fusion(f32[8,8,128]{2,1,0:T(8,128)S(1)} %get-tuple-element.99, f32[8,8,128]{2,1,0:T(8,128)S(1)} %get-tuple-element.155, f32[8,8,128]{2,1,0:T(8,128)S(1)} %get-tuple-element.108, ...), kind=kLoop, calls=%fused_computation.29 | loop fusion | flops 67076096 | bytes 786944 | tf_op jit(solution)/shard_map/reduce_sum | solution.py:63
  371.6 21.8 %multiply_reduce_fusion.5 = (f32[8,8,128]{2,1,0:T(8,128)S(1)}, f32[8,8,128]{2,1,0:T(8,128)S(1)}, f32[8,8,128]{2,1,0:T(8,128)S(1)}, f32[8,8,128]{2,1,0:T(8,128)S(1)}) fusion(f32[8,8,128]{2,1,0:T(8,128)S(1)} %get-tuple-element.104, f32[8,8,128]{2,1,0:T(8,128)S(1)} %get-tuple-element.155, f32[8,8,128]{2,1,0:T(8,128)S(1)} %get-tuple-element.125, ...), kind=kLoop, calls=%fused_computation.24 | loop fusion | flops 67076096 | bytes 786944 | tf_op jit(solution)/shard_map/reduce_sum | solution.py:63
  393.4 22.0 %multiply_reduce_fusion.1 = (f32[8,8,128]{2,1,0:T(8,128)S(1)}, f32[8,8,128]{2,1,0:T(8,128)S(1)}, f32[8,8,128]{2,1,0:T(8,128)S(1)}, f32[8,8,128]{2,1,0:T(8,128)S(1)}) fusion(f32[8,8,128]{2,1,0:T(8,128)S(1)} %get-tuple-element.97, f32[8,8,128]{2,1,0:T(8,128)S(1)} %get-tuple-element.155, f32[8,8,128]{2,1,0:T(8,128)S(1)} %get-tuple-element.113, ...), kind=kLoop, calls=%fused_computation.14 | loop fusion | flops 67076096 | bytes 786944 | tf_op jit(solution)/shard_map/reduce_sum | solution.py:63
  (131 shorter events, 55.3 us)
Async XLA Ops:
  0.6 20.5 %copy-start.6 = (s32[8,128]{1,0:T(8,128)S(1)}, s32[8,128]{1,0:T(8,128)}, u32[]{:S(2)}) copy-start(s32[8,128]{1,0:T(8,128)} %param.16) | copy-start | bytes 12292
  0.6 20.6 %copy-start.1 = (s32[8,8,9]{2,1,0:T(8,128)S(1)}, s32[8,8,9]{2,1,0:T(8,128)}, u32[]{:S(2)}) copy-start(s32[8,8,9]{2,1,0:T(8,128)} %param.15) | copy-start | bytes 6916
  1.4 117.0 %collective-permute-start.3 = (f32[2,1,8,128]{3,2,1,0:T(8,128)S(1)}, f32[2,1,8,128]{3,2,1,0:T(8,128)S(1)}, u32[]{:S(2)}, u32[]{:S(2)}) collective-permute-start(f32[2,1,8,128]{3,2,1,0:T(8,128)S(1)} %get-tuple-element.171), channel_id=1, source_target_pairs={{0,16},{16,32},{32,48},{48,64},{64,80},{80,96},{96,112},{1,17},{17... | collective-permute-start | bytes 24584 | tf_op jit(solution)/shard_map/ppermute | solution.py:26
  4.6 115.8 %collective-permute-start.4 = (f32[2,1,8,128]{3,2,1,0:T(8,128)S(1)}, f32[2,1,8,128]{3,2,1,0:T(8,128)S(1)}, u32[]{:S(2)}, u32[]{:S(2)}) collective-permute-start(f32[2,1,8,128]{3,2,1,0:T(8,128)S(1)} %get-tuple-element.170), channel_id=1, source_target_pairs={{16,0},{32,16},{48,32},{64,48},{80,64},{96,80},{112,96},{17,1},{33... | collective-permute-start | bytes 24584 | tf_op jit(solution)/shard_map/ppermute | solution.py:28
  9.5 112.9 %collective-permute-start = (f32[2,1,8,128]{3,2,1,0:T(8,128)S(1)}, f32[2,1,8,128]{3,2,1,0:T(8,128)S(1)}, u32[]{:S(2)}, u32[]{:S(2)}) collective-permute-start(f32[2,1,8,128]{3,2,1,0:T(8,128)S(1)} %get-tuple-element.169), channel_id=1, source_target_pairs={{0,16},{16,32},{32,48},{48,64},{64,80},{80,96},{96,112},{1,17},{17... | collective-permute-start | bytes 24584 | tf_op jit(solution)/shard_map/ppermute | solution.py:26
  12.2 66.8 %collective-permute-start.13 = (f32[2,512]{1,0:T(2,128)S(1)}, f32[2,512]{1,0:T(2,128)S(1)}, u32[]{:S(2)}, u32[]{:S(2)}) collective-permute-start(f32[2,512]{1,0:T(2,128)S(1)} %get-tuple-element.95), channel_id=1, source_target_pairs={{16,0},{32,16},{48,32},{64,48},{80,64},{96,80},{112,96},{17,1},{33... | collective-permute-start | bytes 12296 | tf_op jit(solution)/shard_map/ppermute | solution.py:28
  17.6 61.3 %collective-permute-start.12 = (f32[2,512]{1,0:T(2,128)S(1)}, f32[2,512]{1,0:T(2,128)S(1)}, u32[]{:S(2)}, u32[]{:S(2)}) collective-permute-start(f32[2,512]{1,0:T(2,128)S(1)} %get-tuple-element.94), channel_id=1, source_target_pairs={{0,16},{16,32},{32,48},{48,64},{64,80},{80,96},{96,112},{1,17},{17... | collective-permute-start | bytes 12296 | tf_op jit(solution)/shard_map/ppermute | solution.py:26
  21.3 16.9 %copy-start = (f32[128,512]{1,0:T(8,128)S(1)}, f32[128,512]{1,0:T(8,128)}, u32[]{:S(2)}) copy-start(f32[128,512]{1,0:T(8,128)} %param.18) | copy-start | bytes 786436
  44.4 22.2 %copy-start.8 = (s32[4]{0:T(128)S(1)}, s32[4]{0:T(128)}, u32[]{:S(2)}) copy-start(s32[4]{0:T(128)} %constant.374.clone.1) | copy-start | bytes 52
  79.0 25.6 %collective-permute-start.15 = (f32[132,2]{1,0:T(8,128)S(1)}, f32[132,2]{1,0:T(8,128)S(1)}, u32[]{:S(2)}, u32[]{:S(2)}) collective-permute-start(f32[132,2]{1,0:T(8,128)S(1)} %get-tuple-element.91), channel_id=1, source_target_pairs={{1,0},{2,1},{3,2},{4,3},{5,4},{6,5},{7,6},{8,7},{9,8},{10,9},{11,1... | collective-permute-start | bytes 3176 | tf_op jit(solution)/shard_map/ppermute | solution.py:28
  93.3 13.6 %collective-permute-start.14 = (f32[132,2]{1,0:T(8,128)S(1)}, f32[132,2]{1,0:T(8,128)S(1)}, u32[]{:S(2)}, u32[]{:S(2)}) collective-permute-start(f32[132,2]{1,0:T(8,128)S(1)} %get-tuple-element.90), channel_id=1, source_target_pairs={{0,1},{1,2},{2,3},{3,4},{4,5},{5,6},{6,7},{7,8},{8,9},{9,10},{10,1... | collective-permute-start | bytes 3176 | tf_op jit(solution)/shard_map/ppermute | solution.py:26
  104.6 17.8 %collective-permute-start.1 = (f32[2,1,8,128]{3,2,1,0:T(8,128)S(1)}, f32[2,1,8,128]{3,2,1,0:T(8,128)S(1)}, u32[]{:S(2)}, u32[]{:S(2)}) collective-permute-start(f32[2,1,8,128]{3,2,1,0:T(8,128)S(1)} %get-tuple-element.168), channel_id=1, source_target_pairs={{16,0},{32,16},{48,32},{64,48},{80,64},{96,80},{112,96},{17,1},{33... | collective-permute-start | bytes 24584 | tf_op jit(solution)/shard_map/ppermute | solution.py:28
  114.6 17.1 %collective-permute-start.17 = (f32[2,512]{1,0:T(2,128)S(1)}, f32[2,512]{1,0:T(2,128)S(1)}, u32[]{:S(2)}, u32[]{:S(2)}) collective-permute-start(f32[2,512]{1,0:T(2,128)S(1)} %get-tuple-element.93), channel_id=1, source_target_pairs={{16,0},{32,16},{48,32},{64,48},{80,64},{96,80},{112,96},{17,1},{33... | collective-permute-start | bytes 12296 | tf_op jit(solution)/shard_map/ppermute | solution.py:28
  118.4 13.3 %collective-permute-start.16 = (f32[2,512]{1,0:T(2,128)S(1)}, f32[2,512]{1,0:T(2,128)S(1)}, u32[]{:S(2)}, u32[]{:S(2)}) collective-permute-start(f32[2,512]{1,0:T(2,128)S(1)} %get-tuple-element.92), channel_id=1, source_target_pairs={{0,16},{16,32},{32,48},{48,64},{64,80},{80,96},{96,112},{1,17},{17... | collective-permute-start | bytes 12296 | tf_op jit(solution)/shard_map/ppermute | solution.py:26
  120.4 67.6 %collective-permute-start.7 = (f32[2,10,1,128]{3,2,1,0:T(1,128)S(1)}, f32[2,10,1,128]{3,2,1,0:T(1,128)S(1)}, u32[]{:S(2)}, u32[]{:S(2)}) collective-permute-start(f32[2,10,1,128]{3,2,1,0:T(1,128)S(1)} %get-tuple-element.139), channel_id=1, source_target_pairs={{1,0},{2,1},{3,2},{4,3},{5,4},{6,5},{7,6},{8,7},{9,8},{10,9},{11,1... | collective-permute-start | bytes 30728 | tf_op jit(solution)/shard_map/ppermute | solution.py:28
  122.5 65.6 %collective-permute-start.6 = (f32[2,10,1,128]{3,2,1,0:T(1,128)S(1)}, f32[2,10,1,128]{3,2,1,0:T(1,128)S(1)}, u32[]{:S(2)}, u32[]{:S(2)}) collective-permute-start(f32[2,10,1,128]{3,2,1,0:T(1,128)S(1)} %get-tuple-element.137), channel_id=1, source_target_pairs={{1,0},{2,1},{3,2},{4,3},{5,4},{6,5},{7,6},{8,7},{9,8},{10,9},{11,1... | collective-permute-start | bytes 30728 | tf_op jit(solution)/shard_map/ppermute | solution.py:28
  124.4 41.6 %collective-permute-start.5 = (f32[2,10,1,128]{3,2,1,0:T(1,128)S(1)}, f32[2,10,1,128]{3,2,1,0:T(1,128)S(1)}, u32[]{:S(2)}, u32[]{:S(2)}) collective-permute-start(f32[2,10,1,128]{3,2,1,0:T(1,128)S(1)} %get-tuple-element.138), channel_id=1, source_target_pairs={{0,1},{1,2},{2,3},{3,4},{4,5},{5,6},{6,7},{7,8},{8,9},{9,10},{10,1... | collective-permute-start | bytes 30728 | tf_op jit(solution)/shard_map/ppermute | solution.py:26
  131.8 31.3 %collective-permute-start.19 = (f32[132,2]{1,0:T(8,128)S(1)}, f32[132,2]{1,0:T(8,128)S(1)}, u32[]{:S(2)}, u32[]{:S(2)}) collective-permute-start(f32[132,2]{1,0:T(8,128)S(1)} %get-tuple-element.89), channel_id=1, source_target_pairs={{1,0},{2,1},{3,2},{4,3},{5,4},{6,5},{7,6},{8,7},{9,8},{10,9},{11,1... | collective-permute-start | bytes 3176 | tf_op jit(solution)/shard_map/ppermute | solution.py:28
  133.7 31.6 %collective-permute-start.18 = (f32[132,2]{1,0:T(8,128)S(1)}, f32[132,2]{1,0:T(8,128)S(1)}, u32[]{:S(2)}, u32[]{:S(2)}) collective-permute-start(f32[132,2]{1,0:T(8,128)S(1)} %get-tuple-element.88), channel_id=1, source_target_pairs={{0,1},{1,2},{2,3},{3,4},{4,5},{5,6},{6,7},{7,8},{8,9},{9,10},{10,1... | collective-permute-start | bytes 3176 | tf_op jit(solution)/shard_map/ppermute | solution.py:26
  163.1 3.1 collective-permute-start.2
  244.5 52.6 %collective-permute-start.9 = (f32[2,1,8,128]{3,2,1,0:T(8,128)S(1)}, f32[2,1,8,128]{3,2,1,0:T(8,128)S(1)}, u32[]{:S(2)}, u32[]{:S(2)}) collective-permute-start(f32[2,1,8,128]{3,2,1,0:T(8,128)S(1)} %get-tuple-element.157), channel_id=1, source_target_pairs={{16,0},{32,16},{48,32},{64,48},{80,64},{96,80},{112,96},{17,1},{33... | collective-permute-start | bytes 24584 | tf_op jit(solution)/shard_map/ppermute | solution.py:28
  250.0 47.1 %collective-permute-start.8 = (f32[2,1,8,128]{3,2,1,0:T(8,128)S(1)}, f32[2,1,8,128]{3,2,1,0:T(8,128)S(1)}, u32[]{:S(2)}, u32[]{:S(2)}) collective-permute-start(f32[2,1,8,128]{3,2,1,0:T(8,128)S(1)} %get-tuple-element.156), channel_id=1, source_target_pairs={{0,16},{16,32},{32,48},{48,64},{64,80},{80,96},{96,112},{1,17},{17... | collective-permute-start | bytes 24584 | tf_op jit(solution)/shard_map/ppermute | solution.py:26
  297.1 41.2 %collective-permute-start.11 = (f32[2,10,1,128]{3,2,1,0:T(1,128)S(1)}, f32[2,10,1,128]{3,2,1,0:T(1,128)S(1)}, u32[]{:S(2)}, u32[]{:S(2)}) collective-permute-start(f32[2,10,1,128]{3,2,1,0:T(1,128)S(1)} %get-tuple-element.134), channel_id=1, source_target_pairs={{1,0},{2,1},{3,2},{4,3},{5,4},{6,5},{7,6},{8,7},{9,8},{10,9},{11,1... | collective-permute-start | bytes 30728 | tf_op jit(solution)/shard_map/ppermute | solution.py:28
  310.1 28.3 %collective-permute-start.10 = (f32[2,10,1,128]{3,2,1,0:T(1,128)S(1)}, f32[2,10,1,128]{3,2,1,0:T(1,128)S(1)}, u32[]{:S(2)}, u32[]{:S(2)}) collective-permute-start(f32[2,10,1,128]{3,2,1,0:T(1,128)S(1)} %get-tuple-element.135), channel_id=1, source_target_pairs={{0,1},{1,2},{2,3},{3,4},{4,5},{5,6},{6,7},{7,8},{8,9},{9,10},{10,1... | collective-permute-start | bytes 30728 | tf_op jit(solution)/shard_map/ppermute | solution.py:26
  (5 other events, 12.6 us)
